TPU v7x, 32 devices: a whole 2x2x4 slice. The times are simulated.
32 devices in a mesh: expert: 4 (over z), batch: 8 (over y, x, core).
Axes of the slice: x: 2, y: 2, z: 4, core: 2. Of those that a mesh axis runs over, the one named last changes fastest.
Arguments:
- tokens: bfloat16 [32, 1024, 768], P(('expert', 'batch')), may hold values from -6 to 6
- lengths: int32 [32], P(('expert', 'batch')), may hold values from 64 to 1024, as said below
- routes: int32 [32, 1024, 2], P(('expert', 'batch')), may hold values from 0 to 7, as said below
- ln1_gain: float32 [768], replicated, may hold values from 0.5 to 1.5
- ln1_bias: float32 [768], replicated, may hold values from -1.5 to 1.5
- ln2_gain: float32 [768], replicated, may hold values from 0.5 to 1.5
- ln2_bias: float32 [768], replicated, may hold values from -1.5 to 1.5
- w_qkv: bfloat16 [768, 2304], replicated, may hold values from -0.21875 to 0.21875
- w_proj: bfloat16 [768, 768], replicated, may hold values from -1.25 to 1.25
- w_router: bfloat16 [768, 8], replicated, may hold values from -0.15625 to 0.15625
- old_in: bfloat16 [4, 768, 3072], P('expert', 'batch'), may hold values from -0.21875 to 0.21875
- old_out: bfloat16 [4, 3072, 768], P('expert', 'batch'), may hold values from -0.109375 to 0.109375
- new_in: bfloat16 [4, 768, 3072], P('expert', 'batch'), may hold values from -0.21875 to 0.21875
- new_out: bfloat16 [4, 3072, 768], P('expert', 'batch'), may hold values from -0.109375 to 0.109375
- cotangent: bfloat16 [32, 1024, 768], P(('expert', 'batch')), may hold values from -6 to 6
Outputs:
- output: float32 [32, 1024, 768], P(('expert', 'batch'))
- input_grad: float32 [32, 1024, 768], P(('expert', 'batch'))
- ln1_gain_grad: float32 [768], replicated
- ln1_bias_grad: float32 [768], replicated
- ln2_gain_grad: float32 [768], replicated
- ln2_bias_grad: float32 [768], replicated
- qkv_grad: float32 [768, 2304], replicated
- proj_grad: float32 [768, 768], replicated
- router_grad: float32 [768, 8], replicated
- new_in_grad: float32 [4, 768, 3072], P('expert', 'batch')
- new_out_grad: float32 [4, 3072, 768], P('expert', 'batch')
Inputs may be any that keep to these rules, and one draw needn't show every extreme that they name: Positions lengths[r] and beyond of row r are padding. In every draw some row has 1024 tokens and some row 64. `routes`: the two experts of one token always differ. Across the tokens of a sequence row the same expert is named many times, and some experts are named more often than others.
All inputs are finite; a program needn't handle non-finite values.
Results may differ from a plain program's by a relative error of at most 0.012.
Values may be sent and summed in bfloat16 or wider, within the bound.
No kernel may reach another device: no remote copies, remote signals or barrier semaphores. Data moves between devices by JAX's collectives and lax.ppermute only.
A program may use at most 320 MiB of HBM per device.

v0:
```python
import math
import jax
import jax.numpy as jnp
from jax import lax
from jax.sharding import PartitionSpec as P

HEADS = 12
HEAD_DIM = 64
norm_eps = 1e-05
masked_value = -1e30


def layer_norm(field_in, gain_vec, bias_vec):
    row_mean = jnp.mean(field_in, axis=-1, keepdims=True)
    centred = field_in - row_mean
    row_var = jnp.mean(centred * centred, axis=-1, keepdims=True)
    return centred * lax.rsqrt(row_var + norm_eps) * gain_vec + bias_vec


def gelu_tanh(field_in):
    inner_arg = 0.7978845608028654 * (field_in + 0.044715 * field_in * field_in * field_in)
    return 0.5 * field_in * (1.0 + jnp.tanh(inner_arg))


def rank_pairs(route_row, length, experts, capacity):
    seq_len = route_row.shape[0]
    pair_expert = jnp.transpose(route_row).reshape(2 * seq_len)
    live_pair = jnp.tile(jnp.arange(seq_len, dtype=jnp.int32) < length, 2)
    one_hot = (pair_expert[:, None] == jnp.arange(experts, dtype=jnp.int32)[None, :]).astype(
        jnp.int32
    ) * live_pair[:, None].astype(jnp.int32)
    earlier = jnp.cumsum(one_hot, axis=0, dtype=jnp.int32) - one_hot
    pair_rank = jnp.sum(earlier * one_hot, axis=1, dtype=jnp.int32)
    kept_pair = live_pair & (pair_rank < capacity)
    return (
        jnp.transpose(pair_rank.reshape(2, seq_len)),
        jnp.transpose(kept_pair.reshape(2, seq_len)),
    )


def buffer_row(expert_ids, experts, group_size):
    half_count = experts // 2
    per_device = half_count // group_size
    is_new = expert_ids >= half_count
    within = jnp.where(is_new, expert_ids - half_count, expert_ids)
    extra = jnp.where(is_new, per_device, 0).astype(jnp.int32)
    return within // per_device * (2 * per_device) + extra + within % per_device


def expert_hidden(buffer_rows, weights_in):
    pre_act = jnp.einsum(
        "slcd,ldf->slcf", buffer_rows, weights_in, preferred_element_type=jnp.float32
    )
    return (pre_act, gelu_tanh(pre_act).astype(jnp.bfloat16))


def expert_output(hidden, weights_out):
    return jnp.einsum("slcf,lfd->slcd", hidden, weights_out, preferred_element_type=jnp.float32)


def expert_back(pre_act, grads_out, weights_out):
    hid_grad = jnp.einsum(
        "slcd,lfd->slcf", grads_out, weights_out, preferred_element_type=jnp.float32
    )
    unused, gelu_back = jax.vjp(gelu_tanh, pre_act)
    return gelu_back(hid_grad)[0].astype(jnp.bfloat16)


def row_grads_of(pre_grad, weights_in):
    return jnp.einsum("slcf,ldf->slcd", pre_grad, weights_in, preferred_element_type=jnp.float32)


def body(
    tokens,
    lengths,
    routes,
    ln1_gain,
    ln1_bias,
    ln2_gain,
    ln2_bias,
    w_qkv,
    w_proj,
    w_router,
    old_in,
    old_out,
    new_in,
    new_out,
    cotangent,
):
    group_size = lax.axis_size("expert")
    inputs = tokens[0].astype(jnp.float32)
    seq_len = inputs.shape[0]
    model_width = inputs.shape[1]
    experts = w_router.shape[1]
    local_count = experts // group_size
    old_count = old_in.shape[0]
    capacity = max(4, seq_len // experts)
    buffer_size = experts * capacity
    score_scale = 1.0 / math.sqrt(HEAD_DIM)
    length = lengths[0]
    route_row = routes[0]
    block_rows = min(512, seq_len)
    blocks = seq_len // block_rows
    normed1, back_norm1 = jax.vjp(layer_norm, inputs, ln1_gain, ln1_bias)
    normed1_low = normed1.astype(jnp.bfloat16)
    qkv_low = jnp.dot(normed1_low, w_qkv, preferred_element_type=jnp.float32).astype(jnp.bfloat16)
    queries = qkv_low[:, :model_width].reshape(seq_len, HEADS, HEAD_DIM)
    key_rows = qkv_low[:, model_width : 2 * model_width].reshape(seq_len, HEADS, HEAD_DIM)
    value_rows = qkv_low[:, 2 * model_width :].reshape(seq_len, HEADS, HEAD_DIM)
    key_pos = jnp.arange(seq_len, dtype=jnp.int32)

    def block_scores(row_start, query_block):
        raw_scores = (
            jnp.einsum("qhd,khd->hqk", query_block, key_rows, preferred_element_type=jnp.float32)
            * score_scale
        )
        query_pos = row_start + jnp.arange(query_block.shape[0], dtype=jnp.int32)
        allowed = (key_pos[None, :] <= query_pos[:, None]) & (key_pos[None, :] < length)
        return jnp.where(allowed[None], raw_scores, masked_value)

    mixed_parts = []
    lse_parts = []
    for block_index in range(blocks):
        row_start = block_index * block_rows
        scores = block_scores(row_start, queries[row_start : row_start + block_rows])
        row_max = jnp.max(scores, axis=-1, keepdims=True)
        exp_scores = jnp.exp(scores - row_max)
        row_total = jnp.sum(exp_scores, axis=-1, keepdims=True)
        prob_low = (exp_scores / row_total).astype(jnp.bfloat16)
        mixed_parts.append(
            jnp.einsum(
                "hqk,khd->qhd", prob_low, value_rows, preferred_element_type=jnp.float32
            ).astype(jnp.bfloat16)
        )
        lse_parts.append(row_max + jnp.log(row_total))
    mixed_rows = jnp.concatenate(mixed_parts, axis=0).reshape(seq_len, model_width)
    residual = inputs + jnp.dot(mixed_rows, w_proj, preferred_element_type=jnp.float32)
    normed2, back_norm2 = jax.vjp(layer_norm, residual, ln2_gain, ln2_bias)
    normed2_low = normed2.astype(jnp.bfloat16)
    logits = jnp.dot(normed2_low, w_router, preferred_element_type=jnp.float32)
    gate_vals = jax.nn.softmax(jnp.take_along_axis(logits, route_row, axis=1), axis=-1)
    pair_rank, kept_pair = rank_pairs(route_row, length, experts, capacity)
    slot_index = buffer_row(route_row, experts, group_size) * capacity + pair_rank
    target = jnp.where(kept_pair, slot_index, buffer_size).reshape(-1)
    token_ids = jnp.broadcast_to(
        jnp.arange(seq_len, dtype=jnp.int32)[:, None], (seq_len, 2)
    ).reshape(-1)
    source_token = jnp.zeros((buffer_size,), jnp.int32).at[target].set(token_ids, mode="drop")
    slot_gate = (
        jnp.zeros((buffer_size,), jnp.float32).at[target].set(gate_vals.reshape(-1), mode="drop")
    )
    slot_filled = jnp.zeros((buffer_size,), jnp.bool_).at[target].set(True, mode="drop")
    pick_index = jnp.where(kept_pair, slot_index, 0)
    kept_weight = kept_pair.astype(jnp.float32)
    zero_low = jnp.zeros((), jnp.bfloat16)
    send_rows = jnp.where(slot_filled[:, None], normed2_low[source_token], zero_low)
    send_rows = send_rows.reshape(group_size, local_count, capacity, model_width)
    received = lax.all_to_all(send_rows, "expert", split_axis=0, concat_axis=0, tiled=True)
    gathered = (
        lax.all_gather(old_in, "batch", axis=1, tiled=True),
        lax.all_gather(old_out, "batch", axis=1, tiled=True),
        lax.all_gather(new_in, "batch", axis=1, tiled=True),
        lax.all_gather(new_out, "batch", axis=1, tiled=True),
    )
    old_rows = received[:, :old_count]
    new_rows = received[:, old_count:]
    old_pre, old_hid = expert_hidden(old_rows, gathered[0])
    new_pre, new_hid = expert_hidden(new_rows, gathered[2])
    expert_result = jnp.concatenate(
        [expert_output(old_hid, gathered[1]), expert_output(new_hid, gathered[3])], axis=1
    ).astype(jnp.bfloat16)
    returned = lax.all_to_all(
        expert_result, "expert", split_axis=0, concat_axis=0, tiled=True
    ).reshape(buffer_size, model_width)
    picked = returned[pick_index].astype(jnp.float32)
    mixture = jnp.sum((gate_vals * kept_weight)[:, :, None] * picked, axis=1)
    output = residual + mixture
    grad_out = cotangent[0].astype(jnp.float32)
    gate_grad = kept_weight * jnp.sum(grad_out[:, None, :] * picked, axis=-1)
    dchosen = gate_vals * (gate_grad - jnp.sum(gate_vals * gate_grad, axis=-1, keepdims=True))
    columns = jnp.arange(experts, dtype=jnp.int32)
    dlogits = jnp.sum(
        (route_row[:, :, None] == columns[None, None, :]).astype(jnp.float32) * dchosen[:, :, None],
        axis=1,
    ).astype(jnp.bfloat16)
    send_grads = jnp.where(
        slot_filled[:, None],
        (slot_gate[:, None] * grad_out[source_token]).astype(jnp.bfloat16),
        zero_low,
    )
    send_grads = send_grads.reshape(group_size, local_count, capacity, model_width)
    arrived = lax.all_to_all(send_grads, "expert", split_axis=0, concat_axis=0, tiled=True)
    weights_back = (
        lax.all_gather(old_in, "batch", axis=1, tiled=True),
        lax.all_gather(old_out, "batch", axis=1, tiled=True),
        lax.all_gather(new_in, "batch", axis=1, tiled=True),
        lax.all_gather(new_out, "batch", axis=1, tiled=True),
    )
    old_pre, old_hid = expert_hidden(old_rows, weights_back[0])
    new_pre, new_hid = expert_hidden(new_rows, weights_back[2])
    old_dout = arrived[:, :old_count]
    new_dout = arrived[:, old_count:]
    old_dpre = expert_back(old_pre, old_dout, weights_back[1])
    new_dpre = expert_back(new_pre, new_dout, weights_back[3])
    new_out_local = jnp.einsum(
        "slcf,slcd->lfd", new_hid, new_dout, preferred_element_type=jnp.float32
    )
    new_in_local = jnp.einsum(
        "slcd,slcf->ldf", new_rows, new_dpre, preferred_element_type=jnp.float32
    )
    row_grads = jnp.concatenate(
        [row_grads_of(old_dpre, weights_back[0]), row_grads_of(new_dpre, weights_back[2])], axis=1
    ).astype(jnp.bfloat16)
    returned_grads = lax.all_to_all(
        row_grads, "expert", split_axis=0, concat_axis=0, tiled=True
    ).reshape(buffer_size, model_width)
    new_in_grad, new_out_grad = (
        lax.psum_scatter(new_in_local, "batch", scatter_dimension=1, tiled=True),
        lax.psum_scatter(new_out_local, "batch", scatter_dimension=1, tiled=True),
    )
    dnormed2 = jnp.sum(
        kept_weight[:, :, None] * returned_grads[pick_index].astype(jnp.float32), axis=1
    )
    dnormed2 = dnormed2 + jnp.dot(dlogits, w_router.T, preferred_element_type=jnp.float32)
    router_local = jnp.dot(normed2_low.T, dlogits, preferred_element_type=jnp.float32)
    dresid_norm, gain2_local, bias2_local = back_norm2(dnormed2)
    dresid = grad_out + dresid_norm
    attn_grad = dresid.astype(jnp.bfloat16)
    proj_local = jnp.dot(mixed_rows.T, attn_grad, preferred_element_type=jnp.float32)
    dmixed = (
        jnp.dot(attn_grad, w_proj.T, preferred_element_type=jnp.float32)
        .astype(jnp.bfloat16)
        .reshape(seq_len, HEADS, HEAD_DIM)
    )
    key_grads = jnp.zeros((seq_len, HEADS, HEAD_DIM), jnp.float32)
    value_grads = jnp.zeros((seq_len, HEADS, HEAD_DIM), jnp.float32)
    dquery_parts = []
    for block_index in range(blocks):
        row_start = block_index * block_rows
        query_block = queries[row_start : row_start + block_rows]
        grad_block = dmixed[row_start : row_start + block_rows]
        scores = block_scores(row_start, query_block)
        probs = jnp.exp(scores - lse_parts[block_index])
        dprobs = jnp.einsum(
            "qhd,khd->hqk", grad_block, value_rows, preferred_element_type=jnp.float32
        )
        dscores = (probs * (dprobs - jnp.sum(probs * dprobs, axis=-1, keepdims=True))).astype(
            jnp.bfloat16
        )
        dquery_parts.append(
            jnp.einsum("hqk,khd->qhd", dscores, key_rows, preferred_element_type=jnp.float32)
            * score_scale
        )
        key_grads = (
            key_grads
            + jnp.einsum("hqk,qhd->khd", dscores, query_block, preferred_element_type=jnp.float32)
            * score_scale
        )
        value_grads = value_grads + jnp.einsum(
            "hqk,qhd->khd",
            probs.astype(jnp.bfloat16),
            grad_block,
            preferred_element_type=jnp.float32,
        )
    query_grads = jnp.concatenate(dquery_parts, axis=0)
    qkv_grads = jnp.concatenate(
        [
            query_grads.reshape(seq_len, model_width),
            key_grads.reshape(seq_len, model_width),
            value_grads.reshape(seq_len, model_width),
        ],
        axis=1,
    ).astype(jnp.bfloat16)
    qkv_local = jnp.dot(normed1_low.T, qkv_grads, preferred_element_type=jnp.float32)
    dnormed1 = jnp.dot(qkv_grads, w_qkv.T, preferred_element_type=jnp.float32)
    dinput_norm, gain1_local, bias1_local = back_norm1(dnormed1)
    input_grad = dresid + dinput_norm
    summed = lax.psum(
        (qkv_local, proj_local, router_local, gain1_local, bias1_local, gain2_local, bias2_local),
        ("expert", "batch"),
    )
    return (
        output[None],
        input_grad[None],
        summed[3],
        summed[4],
        summed[5],
        summed[6],
        summed[0],
        summed[1],
        summed[2],
        new_in_grad,
        new_out_grad,
    )


def solution(mesh):
    placed = (
        P(("expert", "batch"), None, None),
        P(("expert", "batch")),
        P(("expert", "batch"), None, None),
        P(),
        P(),
        P(),
        P(),
        P(),
        P(),
        P(),
        P("expert", "batch", None),
        P("expert", "batch", None),
        P("expert", "batch", None),
        P("expert", "batch", None),
        P(("expert", "batch"), None, None),
    )
    return jax.shard_map(
        body,
        mesh=mesh,
        in_specs=placed,
        out_specs=(
            P(("expert", "batch"), None, None),
            P(("expert", "batch"), None, None),
            P(),
            P(),
            P(),
            P(),
            P(),
            P(),
            P(),
            P("expert", "batch", None),
            P("expert", "batch", None),
        ),
        check_vma=False,
    )
```

profile of v0, /device:TPU:0, one launch (start us, length us, event | category | flops | bytes accessed | tf_op | source)
XLA Modules:
  0.0 1011.6 jit_solution(11103398749579291212)
XLA Ops:
  44.8 9.4 scatter_custom_fusion
  66.8 15.3 %fusion.13 = (f32[12,512]{1,0:T(8,128)S(1)}, f32[12,512,1024]{2,1,0:T(8,128)}) fusion(pred[512,1024]{1,0:T(8,128)(4,1)} %get-tuple-element.111, bf16[512,12,64]{0,2,1:T(8,128)(2,1)} %bitcast.415, bf16[1024,12,64]{0,2,1:T(8,128)(2,1)} %bitcast.406), kind=kOutput, calls=%fused_computation.37 | convolution fusion | flops 824174592 | bytes 28073984 | tf_op jit(solution)/shard_map/qhd,khd->hqk/dot_general | solution.py:114
  82.1 12.5 %fusion.1 = f32[12,512]{1,0:T(8,128)S(1)} fusion(f32[12,512]{1,0:T(8,128)S(1)} %get-tuple-element.112, f32[12,512,1024]{2,1,0:T(8,128)} %get-tuple-element.113, pred[512,1024]{1,0:T(8,128)(4,1)S(1)} %copy-done.17), kind=kLoop, calls=%fused_computation.21 | loop fusion | flops 25159680 | bytes 25739264 | tf_op jit(solution)/shard_map/reduce_sum | solution.py:128
  97.8 9.8 fusion.126
  107.6 12.4 %fusion.12 = (f32[12,512]{1,0:T(8,128)S(1)}, f32[12,512,1024]{2,1,0:T(8,128)}) fusion(pred[512,1024]{1,0:T(8,128)(4,1)} %get-tuple-element.110, bf16[512,12,64]{0,2,1:T(8,128)(2,1)} %bitcast.417, bf16[1024,12,64]{0,2,1:T(8,128)(2,1)S(1)} %bitcast.407), kind=kOutput, calls=%fused_computation.36 | convolution fusion | flops 824174592 | bytes 28073984 | tf_op jit(solution)/shard_map/qhd,khd->hqk/dot_general | solution.py:114
  120.0 14.2 %fusion = f32[12,512]{1,0:T(8,128)S(1)} fusion(f32[12,512]{1,0:T(8,128)S(1)} %get-tuple-element.114, f32[12,512,1024]{2,1,0:T(8,128)} %get-tuple-element.115, pred[512,1024]{1,0:T(8,128)(4,1)} %get-tuple-element.110), kind=kLoop, calls=%fused_computation.20 | loop fusion | flops 25159680 | bytes 25739264 | tf_op jit(solution)/shard_map/reduce_sum | solution.py:128
  136.3 9.6 fusion.125
  152.3 8.7 scatter_custom_fusion.1
  183.4 13.8 %gather_fusion.4 = f32[2048]{0:T(1024)S(1)} fusion(f32[1024,8]{0,1:T(8,128)} %fusion.196, s32[2048]{0:T(1024)S(1)} %reshape.475), kind=kCustom, calls=%fused_computation.4 | custom fusion | bytes 32768 | tf_op jit(solution)/shard_map/jit(take_along_axis)/gather | solution.py:141
  238.3 43.2 %all_to_all.20 = bf16[4,2,128,768]{3,2,1,0:T(8,128)(2,1)} all-to-all(bf16[4,2,128,768]{3,2,1,0:T(8,128)(2,1)S(1)} %get-tuple-element.109), channel_id=1, replica_groups=mesh['expert'=4,'batch'=8] {'expert'}, dimensions={0} | all-to-all | bytes 3145728 | tf_op jit(solution)/shard_map/all_to_all | solution.py:158
  301.9 8.8 fusion.108
  326.8 9.6 fusion.19
  347.4 10.6 %fusion.127 = bf16[4,1,128,768]{3,2,0,1:T(8,128)(2,1)S(1)} fusion(bf16[1,768,3072]{2,1,0:T(8,128)(2,1)} %all-gather.5.cloned.1.call-done, f32[4,128,3072]{2,1,0:T(8,128)} %fusion.52, f32[4,128,3072]{2,1,0:T(8,128)S(1)} %fusion.46), kind=kOutput, calls=%fused_computation.163 | convolution fusion | flops 2454061056 | bytes 18087936 | tf_op jit(solution)/shard_map/slcf,ldf->slcd/dot_general | solution.py:70
  379.6 12.1 %gather_fusion.1 = bf16[2048,768]{1,0:T(8,128)(2,1)} fusion(bf16[1024,768]{1,0:T(8,128)(2,1)} %bitcast.47, s32[2048]{0:T(1024)S(1)} %broadcast_clamp_fusion), kind=kCustom, calls=%fused_computation.1 | custom fusion | bytes 6299648 | tf_op jit(solution)/shard_map/gather | solution.py:175
  391.7 12.6 %all-to-all-done.3 = bf16[4,2,128,768]{3,2,1,0:T(8,128)(2,1)} async-done(((bf16[4,2,128,768]{3,2,1,0:T(8,128)(2,1)}), bf16[4,2,128,768]{3,2,1,0:T(8,128)(2,1)}, u32[]{:S(2)}, u32[]{:S(2)}) %all-to-all-start.3) | async-done | bytes 1572896 | tf_op jit(solution)/shard_map/all_to_all | solution.py:214
  404.3 11.7 %gather_fusion.3 = bf16[2048,768]{1,0:T(8,128)(2,1)} fusion(bf16[1024,768]{1,0:T(8,128)(2,1)} %bitcast.73, s32[2048]{0:T(1024)S(1)} %broadcast_clamp_fusion), kind=kCustom, calls=%fused_computation.3 | custom fusion | bytes 6299648 | tf_op jit(solution)/shard_map/gather | solution.py:222
  423.8 11.2 %multiply_reduce_fusion.3 = f32[1024,768]{1,0:T(8,128)} fusion(f32[1024,2,768]{2,1,0:T(2,128)} %reshape.513, f32[1024,2]{1,0:T(8,128)} %copy.192), kind=kLoop, calls=%fused_computation.73 | loop fusion | flops 2359296 | bytes 9445376 | tf_op jit(solution)/shard_map/reduce_sum | solution.py:221
  446.3 17.2 %multiply_reduce_fusion.2 = (f32[1024,2]{1,0:T(8,128)}, f32[1024,768]{1,0:T(8,128)}) fusion(f32[1024,2,768]{2,1,0:T(2,128)} %reshape.512, f32[1024,768]{1,0:T(8,128)} %copy.196, f32[1024,2]{1,0:T(8,128)} %copy.183), kind=kLoop, calls=%fused_computation.72 | loop fusion | flops 5502976 | bytes 12599296 | tf_op jit(solution)/shard_map/reduce_sum | solution.py:179
  491.6 18.9 %multiply_reduce_fusion.1 = (f32[12,512]{1,0:T(8,128)}, f32[12,512,1024]{2,1,0:T(8,128)}) fusion(f32[12,512]{1,0:T(8,128)} %log_add_fusion.1, f32[12,512,1024]{2,1,0:T(8,128)} %get-tuple-element.115, pred[512,1024]{1,0:T(8,128)(4,1)} %get-tuple-element.110, bf16[512,12,64]{0,2,1:T(8,128)(2,1)} %bitcast.422, bf16[1024,12,64]{0,2,1:T(8,128)(2,1)} %bitcast.412), kind=kOutput, calls=%fused_computation.12 | convolution fusion | flops 836757504 | bytes 53264384 | tf_op jit(solution)/shard_map/qhd,khd->hqk/dot_general | solution.py:244
  510.5 22.7 %multiply_convert_fusion.1 = bf16[12,512,1024]{2,1,0:T(8,128)(2,1)} fusion(f32[12,512,1024]{2,1,0:T(8,128)} %get-tuple-element.120, f32[12,512]{1,0:T(8,128)} %get-tuple-element.119, f32[12,512]{1,0:T(8,128)} %log_add_fusion.1, f32[12,512,1024]{2,1,0:T(8,128)} %get-tuple-element.115, pred[512,1024]{1,0:T(8,128)(4,1)} %get-tuple-element.110), kind=kLoop, calls=%fused_computation.11 | loop fusion | flops 37748736 | bytes 63488000 | tf_op jit(solution)/shard_map/convert_element_type | solution.py:247
  533.2 9.5 fusion.123
  551.4 13.1 %fusion.4 = f32[12,64,1024]{2,1,0:T(8,128)} fusion(bf16[512,12,64]{0,2,1:T(8,128)(2,1)S(1)} %bitcast.425, f32[12,512]{1,0:T(8,128)S(1)} %copy-done.36, f32[12,512,1024]{2,1,0:T(8,128)} %get-tuple-element.113, pred[512,1024]{1,0:T(8,128)(4,1)S(1)} %copy-done.18), kind=kOutput, calls=%fused_computation.24 | convolution fusion | flops 830472192 | bytes 29646848 | tf_op jit(solution)/shard_map/hqk,qhd->khd/dot_general | solution.py:259
  564.4 18.9 %multiply_reduce_fusion = (f32[12,512]{1,0:T(8,128)}, f32[12,512,1024]{2,1,0:T(8,128)}) fusion(f32[12,512]{1,0:T(8,128)} %log_add_fusion, f32[12,512,1024]{2,1,0:T(8,128)} %get-tuple-element.113, pred[512,1024]{1,0:T(8,128)(4,1)} %get-tuple-element.111, bf16[512,12,64]{0,2,1:T(8,128)(2,1)} %bitcast.424, bf16[1024,12,64]{0,2,1:T(8,128)(2,1)} %bitcast.413), kind=kOutput, calls=%fused_computation.9 | convolution fusion | flops 836757504 | bytes 53264384 | tf_op jit(solution)/shard_map/qhd,khd->hqk/dot_general | solution.py:244
  583.3 13.2 %add_convert_fusion = bf16[12,64,1024]{2,1,0:T(8,128)(2,1)S(1)} fusion(f32[12,64,1024]{2,1,0:T(8,128)} %fusion.4, bf16[512,12,64]{0,2,1:T(8,128)(2,1)} %bitcast.423, f32[12,512]{1,0:T(8,128)} %log_add_fusion.1, f32[12,512,1024]{2,1,0:T(8,128)} %get-tuple-element.115, pred[512,1024]{1,0:T(8,128)(4,1)} %get-tuple-element.110), kind=kOutput, calls=%fused_computation.122 | convolution fusion | flops 832045056 | bytes 31219712 | tf_op jit(solution)/shard_map/hqk,qhd->khd/dot_general | solution.py:259
  596.6 21.9 %multiply_convert_fusion = bf16[12,512,1024]{2,1,0:T(8,128)(2,1)} fusion(f32[12,512,1024]{2,1,0:T(8,128)} %get-tuple-element.122, f32[12,512]{1,0:T(8,128)S(1)} %copy-done.42, f32[12,512]{1,0:T(8,128)S(1)} %copy-done.37, f32[12,512,1024]{2,1,0:T(8,128)} %get-tuple-element.113, pred[512,1024]{1,0:T(8,128)(4,1)S(1)} %copy-done.19), kind=kLoop, calls=%fused_computation.8 | loop fusion | flops 37748736 | bytes 63488000 | tf_op jit(solution)/shard_map/convert_element_type | solution.py:247
  618.5 8.6 fusion.124
  643.8 9.9 convolution_bitcast_fusion
  666.1 8.7 fusion.195
  693.5 40.5 %all-reduce = (f32[768]{0:T(1024)}, f32[768]{0:T(1024)}, f32[768]{0:T(1024)}, f32[768]{0:T(1024)}, f32[768,8]{0,1:T(8,128)}) all-reduce(f32[768]{0:T(1024)} %get-tuple-element.81, f32[768]{0:T(1024)} %get-tuple-element.123, f32[768]{0:T(1024)} %get-tuple-element.77, ...), channel_id=1, replica_groups=mesh['expert'=4,'batch'=8] {'expert','batch'}, use_global_device_ids=true, to_apply=%region_28.29 | all-reduce | flops 9216 | bytes 73728 | tf_op jit(solution)/shard_map/psum | solution.py:278
  734.0 100.6 %all-reduce.4.cloned.1.call-done = (f32[768,2304]{1,0:T(8,128)}, f32[768,768]{1,0:T(8,128)}) async-done(((f32[768,2304]{1,0:T(8,128)}, f32[768,768]{1,0:T(8,128)}), (f32[768,2304]{1,0:T(8,128)}, f32[768,768]{1,0:T(8,128)})) %all-reduce.4.cloned.1.call-update) | async-done | bytes 9437200 | tf_op jit(solution)/shard_map/psum | solution.py:278
  834.6 80.8 %reduce-scatter.5.cloned.1.call-done = f32[1,384,768]{2,1,0:T(8,128)} async-done(((f32[1,3072,768]{2,1,0:T(8,128)}), f32[1,384,768]{2,1,0:T(8,128)}) %reduce-scatter.5.cloned.1.call-update) | async-done | bytes 1179664 | tf_op jit(solution)/shard_map/reduce_scatter | solution.py:219
  915.4 80.9 %reduce-scatter.3.cloned.1.call-done = f32[1,96,3072]{2,1,0:T(8,128)} async-done(((f32[1,768,3072]{2,1,0:T(8,128)}), f32[1,96,3072]{2,1,0:T(8,128)}) %reduce-scatter.3.cloned.1.call-update) | async-done | bytes 1179664 | tf_op jit(solution)/shard_map/reduce_scatter | solution.py:218
  (284 shorter events, 304.6 us)
Async XLA Ops:
  7.2 10.3 %copy-start = (bf16[768,2304]{1,0:T(8,128)(2,1)S(1)}, bf16[768,2304]{1,0:T(8,128)(2,1)}, u32[]{:S(2)}) copy-start(bf16[768,2304]{1,0:T(8,128)(2,1)} %param.22) | copy-start | bytes 10616836
  7.2 279.0 %all-gather.9.cloned.1.call-start = ((), (), s32[]{:S(2)}) async-start(), calls=%async_computation.8 | async-start | bytes 5308416 | tf_op jit(solution)/shard_map/all_gather | solution.py:162
  7.9 286.1 %all-gather.5.cloned.1.call-start = ((), (), s32[]{:S(2)}) async-start(), calls=%async_computation.6 | async-start | bytes 5308416 | tf_op jit(solution)/shard_map/all_gather | solution.py:160
  8.7 293.2 %all-gather.11.cloned.1.call-start = ((), (), s32[]{:S(2)}) async-start(), calls=%async_computation.9 | async-start | bytes 5308416 | tf_op jit(solution)/shard_map/all_gather | solution.py:163
  9.4 301.3 %all-gather.7.cloned.1.call-start = ((), (), s32[]{:S(2)}) async-start(), calls=%async_computation.7 | async-start | bytes 5308416 | tf_op jit(solution)/shard_map/all_gather | solution.py:161
  66.8 15.3 %copy-start.17 = (pred[512,1024]{1,0:T(8,128)(4,1)S(1)}, pred[512,1024]{1,0:T(8,128)(4,1)}, u32[]{:S(2)}) copy-start(pred[512,1024]{1,0:T(8,128)(4,1)} %get-tuple-element.111) | copy-start | bytes 1572868
  82.1 12.5 %copy-start.34 = (f32[12,512]{1,0:T(8,128)}, f32[12,512]{1,0:T(8,128)S(1)}, u32[]{:S(2)}) copy-start(f32[12,512]{1,0:T(8,128)S(1)} %get-tuple-element.112) | copy-start | bytes 73732
  82.1 15.7 %copy-start.1 = (f32[12,512,1024]{2,1,0:T(8,128)S(1)}, f32[12,512,1024]{2,1,0:T(8,128)}, u32[]{:S(2)}) copy-start(f32[12,512,1024]{2,1,0:T(8,128)} %get-tuple-element.113) | copy-start | bytes 75497472
  94.6 13.0 %copy-start.43 = (f32[12,512]{1,0:T(8,128)}, f32[12,512]{1,0:T(8,128)S(1)}, u32[]{:S(2)}) copy-start(f32[12,512]{1,0:T(8,128)S(1)} %fusion.1) | copy-start | bytes 73732
  97.8 9.8 copy-start.9
  120.0 14.2 %copy-start.35 = (f32[12,512]{1,0:T(8,128)}, f32[12,512]{1,0:T(8,128)S(1)}, u32[]{:S(2)}) copy-start(f32[12,512]{1,0:T(8,128)S(1)} %get-tuple-element.114) | copy-start | bytes 73732
  120.0 16.2 %copy-start.2 = (f32[12,512,1024]{2,1,0:T(8,128)S(1)}, f32[12,512,1024]{2,1,0:T(8,128)}, u32[]{:S(2)}) copy-start(f32[12,512,1024]{2,1,0:T(8,128)} %get-tuple-element.115) | copy-start | bytes 75497472
  120.0 16.3 %copy-start.20 = (pred[512,1024]{1,0:T(8,128)(4,1)S(1)}, pred[512,1024]{1,0:T(8,128)(4,1)}, u32[]{:S(2)}) copy-start(pred[512,1024]{1,0:T(8,128)(4,1)} %get-tuple-element.110) | copy-start | bytes 1572868
  136.3 9.6 copy-start.44
  281.6 40.7 %all-to-all-start.2 = ((bf16[4,2,128,768]{3,2,1,0:T(8,128)(2,1)}), bf16[4,2,128,768]{3,2,1,0:T(8,128)(2,1)}, u32[]{:S(2)}, u32[]{:S(2)}) async-start(bf16[4,2,128,768]{3,2,1,0:T(8,128)(2,1)} %get-tuple-element.108), calls=%async_computation.2 | async-start | bytes 3145728 | tf_op jit(solution)/shard_map/all_to_all | solution.py:192
  322.3 41.2 %all-to-all-start.1 = ((bf16[4,2,128,768]{3,2,1,0:T(8,128)(2,1)}), bf16[4,2,128,768]{3,2,1,0:T(8,128)(2,1)}, u32[]{:S(2)}, u32[]{:S(2)}) async-start(bf16[4,2,128,768]{3,2,1,0:T(8,128)(2,1)} %copy.188), calls=%async_computation.1 | async-start | bytes 3145728 | tf_op jit(solution)/shard_map/all_to_all | solution.py:172
  359.4 13.8 %copy-start.41 = (pred[2,1024]{1,0:T(4,128)(4,1)S(1)}, pred[2,1024]{1,0:T(4,128)(4,1)}, u32[]{:S(2)}) copy-start(pred[2,1024]{1,0:T(4,128)(4,1)} %copy-done.40) | copy-start | bytes 6148
  359.4 13.8 %copy-start.52 = (f32[1024]{0:T(1024)S(1)}, f32[1024]{0:T(1024)}, u32[]{:S(2)}) copy-start(f32[1024]{0:T(1024)} %copy-done.51) | copy-start | bytes 12292
  363.4 40.9 %all-to-all-start.3 = ((bf16[4,2,128,768]{3,2,1,0:T(8,128)(2,1)}), bf16[4,2,128,768]{3,2,1,0:T(8,128)(2,1)}, u32[]{:S(2)}, u32[]{:S(2)}) async-start(bf16[4,2,128,768]{3,2,1,0:T(8,128)(2,1)} %copy.199), calls=%async_computation.3 | async-start | bytes 3145728 | tf_op jit(solution)/shard_map/all_to_all | solution.py:214
  367.8 466.8 %all-reduce.4.cloned.1.call-start = ((), (), s32[]{:S(2)}) async-start(), calls=%async_computation.12 | async-start | bytes 18874368 | tf_op jit(solution)/shard_map/psum | solution.py:278
  446.3 20.5 %copy-start.33 = (s32[1,1024,2]{1,2,0:T(2,128)S(1)}, s32[1,1024,2]{1,2,0:T(2,128)}, u32[]{:S(2)}) copy-start(s32[1,1024,2]{1,2,0:T(2,128)} %param.17) | copy-start | bytes 24580
  446.3 20.6 %copy-start.46 = (f32[1024]{0:T(1024)S(1)}, f32[1024]{0:T(1024)}, u32[]{:S(2)}) copy-start(f32[1024]{0:T(1024)} %copy-done.45) | copy-start | bytes 12292
  510.5 22.7 %copy-start.10 = (bf16[1024,768]{0,1:T(8,128)(2,1)S(1)}, bf16[1024,768]{0,1:T(8,128)(2,1)}, u32[]{:S(2)}) copy-start(bf16[1024,768]{0,1:T(8,128)(2,1)} %copy.179) | copy-start | bytes 4718596
  533.2 9.5 copy-start.22
  583.3 13.3 %copy-start.19 = (pred[512,1024]{1,0:T(8,128)(4,1)S(1)}, pred[512,1024]{1,0:T(8,128)(4,1)}, u32[]{:S(2)}) copy-start(pred[512,1024]{1,0:T(8,128)(4,1)} %get-tuple-element.111) | copy-start | bytes 1572868
  583.3 13.3 %copy-start.37 = (f32[12,512]{1,0:T(8,128)S(1)}, f32[12,512]{1,0:T(8,128)}, u32[]{:S(2)}) copy-start(f32[12,512]{1,0:T(8,128)} %log_add_fusion) | copy-start | bytes 73732
  583.3 13.3 %copy-start.42 = (f32[12,512]{1,0:T(8,128)S(1)}, f32[12,512]{1,0:T(8,128)}, u32[]{:S(2)}) copy-start(f32[12,512]{1,0:T(8,128)} %get-tuple-element.121) | copy-start | bytes 73732
  596.5 37.8 %copy-start.71 = (bf16[12,64,1024]{2,1,0:T(8,128)(2,1)}, bf16[12,64,1024]{2,1,0:T(8,128)(2,1)S(1)}, u32[]{:S(2)}) copy-start(bf16[12,64,1024]{2,1,0:T(8,128)(2,1)S(1)} %add_convert_fusion) | copy-start | bytes 4718596
  596.6 21.9 %copy-start.11 = (bf16[1024,768]{0,1:T(8,128)(2,1)S(1)}, bf16[1024,768]{0,1:T(8,128)(2,1)}, u32[]{:S(2)}) copy-start(bf16[1024,768]{0,1:T(8,128)(2,1)} %copy.179) | copy-start | bytes 4718596
  618.5 8.7 copy-start.21
  643.8 271.7 %reduce-scatter.5.cloned.1.call-start = ((), (), s32[]{:S(2)}) async-start(), calls=%async_computation.11 | async-start | bytes 10616832 | tf_op jit(solution)/shard_map/reduce_scatter | solution.py:219
  653.7 342.7 %reduce-scatter.3.cloned.1.call-start = ((), (), s32[]{:S(2)}) async-start(), calls=%async_computation.10 | async-start | bytes 10616832 | tf_op jit(solution)/shard_map/reduce_scatter | solution.py:218
  (50 other events, 185.6 us)
Sparse Core Ops, SparseCore 0:
  9.9 41.5 all-gather.8
  53.3 38.7 all-gather.4
  94.1 38.7 all-gather.10
  134.6 38.8 all-gather.6
  643.9 190.6 all-reduce.3
  838.5 76.8 reduce-scatter.4
  919.5 76.8 reduce-scatter.2
where the time goes:
time: 1020 us; the launch traced here: 1010 us
  waiting for transfers between devices  284 us (28%)
  matrix products  264 us (26%)
  local copies, waits for them, and re-layouts  195 us (19%)
  other arithmetic  155 us (15%)
  blocking collectives  83.7 us (8%)
  between operations  16 us (2%)
  starting transfers between devices  13.9 us (1%)
    psum x1, waiting for transfers between devices, body(): lax.psum((qkv_local, proj_local, router_local, gain1_local, bias1_local,...  101 us
    reduce_scatter x1, waiting for transfers between devices, body(): lax.psum_scatter(new_in_local, 'batch', scatter_dimension=1, tiled=True)  80.9 us
    reduce_scatter x1, waiting for transfers between devices, body(): lax.psum_scatter(new_out_local, 'batch', scatter_dimension=1, tiled=True)  80.8 us
    convert_element_type x2, other arithmetic, body(): (probs * (dprobs - jnp.sum(probs * dprobs, axis=-1, keepdims=True))).asty...  44.6 us
    all_to_all x1, blocking collectives, body(): lax.all_to_all(send_rows, 'expert', split_axis=0, concat_axis=0, tiled=True)  43.2 us
    psum x1, blocking collectives, body(): lax.psum((qkv_local, proj_local, router_local, gain1_local, bias1_local,...  40.5 us
    dot_general x2, matrix products, body(): jnp.einsum('qhd,khd->hqk', grad_block, value_rows, preferred_element_type...  37.7 us
    unnamed x154, local copies, waits for them, and re-layouts  37.1 us
  transfers between devices with their start and end apart: 10, of which 6 were waited for; matrix products, arithmetic and copies ran while one was open for 35% of the time, Pallas kernels for 0%

commit v1 on v0

--- a/solution.py
+++ b/solution.py
@@ -8,6 +8,17 @@
 HEAD_DIM = 64
 norm_eps = 1e-05
 masked_value = -1e30
+
+
+def in_blocks(x, dim, count):
+    before, after = (x.shape[:dim], x.shape[dim + 1 :])
+    return jnp.moveaxis(x.reshape(*before, count, -1, *after), dim, 0)
+
+
+def laid_out(pieces, dim):
+    shape = list(pieces.shape[1:])
+    shape[dim] *= pieces.shape[0]
+    return jnp.moveaxis(pieces, 0, dim).reshape(shape)
 
 
 def layer_norm(field_in, gain_vec, bias_vec):
@@ -155,7 +166,14 @@
     zero_low = jnp.zeros((), jnp.bfloat16)
     send_rows = jnp.where(slot_filled[:, None], normed2_low[source_token], zero_low)
     send_rows = send_rows.reshape(group_size, local_count, capacity, model_width)
-    received = lax.all_to_all(send_rows, "expert", split_axis=0, concat_axis=0, tiled=True)
+    size, place = (lax.axis_size("expert"), lax.axis_index("expert"))
+    parts = in_blocks(send_rows, 0, size)
+    outs = [parts[place]]
+    for step in range(1, size):
+        sent = parts[place ^ step]
+        outs.append(lax.ppermute(sent, "expert", [(i, i ^ step) for i in range(size)]))
+    parts = jnp.stack(outs)[place ^ jnp.arange(size)]
+    received = laid_out(parts, 0)
     gathered = (
         lax.all_gather(old_in, "batch", axis=1, tiled=True),
         lax.all_gather(old_out, "batch", axis=1, tiled=True),

time: 1020 us -> 995 us (0.975)
  blocking collectives: 83.7 us -> 40.6 us
    all_to_all x1 -> x0, blocking collectives: 43.2 us -> none  [body(): lax.all_to_all(send_rows, 'expert', split_axis=0, concat_axis=0, tiled=True)]
    unnamed x154 -> x164, local copies, waits for them, and re-layouts: 37.1 us -> 38 us
  transfers between devices with their start and end apart: 10 -> 13, of which waited for: 6 -> 5; matrix products, arithmetic and copies ran while one was open for 35% -> 37% of each run, Pallas kernels for 0% -> 0%
where the time goes in v1:
time: 995 us; the launch traced here: 983 us
  waiting for transfers between devices  280 us (28%)
  matrix products  264 us (27%)
  local copies, waits for them, and re-layouts  203 us (20%)
  other arithmetic  160 us (16%)
  blocking collectives  40.6 us (4%)
  starting transfers between devices  20.7 us (2%)
  between operations  16 us (2%)
    psum x1, waiting for transfers between devices, body(): lax.psum((qkv_local, proj_local, router_local, gain1_local, bias1_local,...  100 us
    reduce_scatter x1, waiting for transfers between devices, body(): lax.psum_scatter(new_in_local, 'batch', scatter_dimension=1, tiled=True)  80.9 us
    reduce_scatter x1, waiting for transfers between devices, body(): lax.psum_scatter(new_out_local, 'batch', scatter_dimension=1, tiled=True)  80.8 us
    convert_element_type x2, other arithmetic, body(): (probs * (dprobs - jnp.sum(probs * dprobs, axis=-1, keepdims=True))).asty...  44.6 us
    psum x1, blocking collectives, body(): lax.psum((qkv_local, proj_local, router_local, gain1_local, bias1_local,...  40.6 us
    unnamed x164, local copies, waits for them, and re-layouts  38 us
    dot_general x2, matrix products, body(): jnp.einsum('qhd,khd->hqk', grad_block, value_rows, preferred_element_type...  37.6 us
    dot_general x2, matrix products, block_scores(): jnp.einsum('qhd,khd->hqk', query_block, key_rows, preferred_element_type=...  26.9 us
  transfers between devices with their start and end apart: 13, of which 5 were waited for; matrix products, arithmetic and copies ran while one was open for 37% of the time, Pallas kernels for 0%

profile of v1, /device:TPU:0, one launch (start us, length us, event | category | flops | bytes accessed | tf_op | source)
XLA Modules:
  0.0 983.5 jit_solution(8285075350827354128)
XLA Ops:
  46.1 14.9 %fusion.13 = (f32[12,512]{1,0:T(8,128)S(1)}, f32[12,512,1024]{2,1,0:T(8,128)}) fusion(pred[512,1024]{1,0:T(8,128)(4,1)S(1)} %get-tuple-element.113, bf16[512,12,64]{0,2,1:T(8,128)(2,1)} %bitcast.428, bf16[1024,12,64]{0,2,1:T(8,128)(2,1)} %bitcast.419), kind=kOutput, calls=%fused_computation.38 | convolution fusion | flops 824174592 | bytes 28073984 | tf_op jit(solution)/shard_map/qhd,khd->hqk/dot_general | solution.py:125
  61.0 12.5 %fusion.1 = f32[12,512]{1,0:T(8,128)S(1)} fusion(f32[12,512]{1,0:T(8,128)S(1)} %get-tuple-element.114, f32[12,512,1024]{2,1,0:T(8,128)} %get-tuple-element.115, pred[512,1024]{1,0:T(8,128)(4,1)S(1)} %get-tuple-element.113), kind=kLoop, calls=%fused_computation.22 | loop fusion | flops 25159680 | bytes 25739264 | tf_op jit(solution)/shard_map/reduce_sum | solution.py:139
  77.3 10.0 %fusion.126 = bf16[512,12,64]{0,2,1:T(8,128)(2,1)} fusion(bf16[1024,12,64]{0,2,1:T(8,128)(2,1)} %bitcast.423, f32[12,512]{1,0:T(8,128)S(1)} %fusion.1, f32[12,512]{1,0:T(8,128)S(1)} %get-tuple-element.114, f32[12,512,1024]{2,1,0:T(8,128)S(1)} %copy-done.1, pred[512,1024]{1,0:T(8,128)(4,1)} %copy-done.17), kind=kOutput, calls=%fused_computation.164 | convolution fusion | flops 837156864 | bytes 28098560 | tf_op jit(solution)/shard_map/hqk,khd->qhd/dot_general | solution.py:142
  87.3 12.0 %fusion.12 = (f32[12,512]{1,0:T(8,128)S(1)}, f32[12,512,1024]{2,1,0:T(8,128)}) fusion(pred[512,1024]{1,0:T(8,128)(4,1)} %get-tuple-element.112, bf16[512,12,64]{0,2,1:T(8,128)(2,1)} %bitcast.430, bf16[1024,12,64]{0,2,1:T(8,128)(2,1)S(1)} %bitcast.420), kind=kOutput, calls=%fused_computation.37 | convolution fusion | flops 824174592 | bytes 28073984 | tf_op jit(solution)/shard_map/qhd,khd->hqk/dot_general | solution.py:125
  99.3 14.2 %fusion = f32[12,512]{1,0:T(8,128)S(1)} fusion(f32[12,512]{1,0:T(8,128)S(1)} %get-tuple-element.116, f32[12,512,1024]{2,1,0:T(8,128)} %get-tuple-element.117, pred[512,1024]{1,0:T(8,128)(4,1)} %get-tuple-element.112), kind=kLoop, calls=%fused_computation.21 | loop fusion | flops 25159680 | bytes 25739264 | tf_op jit(solution)/shard_map/reduce_sum | solution.py:139
  115.8 9.9 %fusion.125 = bf16[512,12,64]{0,2,1:T(8,128)(2,1)} fusion(bf16[1024,12,64]{0,2,1:T(8,128)(2,1)} %bitcast.424, f32[12,512]{1,0:T(8,128)S(1)} %fusion, f32[12,512]{1,0:T(8,128)S(1)} %get-tuple-element.116, f32[12,512,1024]{2,1,0:T(8,128)S(1)} %copy-done.2, pred[512,1024]{1,0:T(8,128)(4,1)S(1)} %copy-done.20), kind=kOutput, calls=%fused_computation.163 | convolution fusion | flops 837156864 | bytes 28098560 | tf_op jit(solution)/shard_map/hqk,khd->qhd/dot_general | solution.py:142
  135.9 10.0 %scatter_custom_fusion = pred[1024]{0:T(1024)(128)(4,1)} fusion(s32[2048]{0:T(1024)} %bitcast.450, pred[2048]{0:T(1024)(128)(4,1)S(1)} %broadcast.370, pred[]{:T(512)} %constant.103.clone.1), kind=kCustom, calls=%fused_computation.244 | custom fusion | bytes 1536 | tf_op jit(solution)/shard_map/scatter | solution.py:163
  149.4 8.7 scatter_custom_fusion.1
  211.1 13.8 %gather_fusion.5 = f32[2048]{0:T(1024)S(1)} fusion(f32[1024,8]{0,1:T(8,128)} %fusion.197, s32[2048]{0:T(1024)S(1)} %reshape.515), kind=kCustom, calls=%fused_computation.5 | custom fusion | bytes 32768 | tf_op jit(solution)/shard_map/jit(take_along_axis)/gather | solution.py:152
  276.3 8.8 fusion.108
  299.8 9.6 fusion.19
  320.3 10.6 %fusion.127 = bf16[4,1,128,768]{3,2,0,1:T(8,128)(2,1)S(1)} fusion(bf16[1,768,3072]{2,1,0:T(8,128)(2,1)} %all-gather.5.cloned.1.call-done, f32[4,128,3072]{2,1,0:T(8,128)} %fusion.52, f32[4,128,3072]{2,1,0:T(8,128)S(1)} %fusion.46), kind=kOutput, calls=%fused_computation.165 | convolution fusion | flops 2454061056 | bytes 18087936 | tf_op jit(solution)/shard_map/slcf,ldf->slcd/dot_general | solution.py:81
  351.6 12.1 %gather_fusion.2 = bf16[2048,768]{1,0:T(8,128)(2,1)} fusion(bf16[1024,768]{1,0:T(8,128)(2,1)} %bitcast.55, s32[2048]{0:T(1024)S(1)} %broadcast_clamp_fusion), kind=kCustom, calls=%fused_computation.2 | custom fusion | bytes 6299648 | tf_op jit(solution)/shard_map/gather | solution.py:193
  363.7 12.6 %all-to-all-done.2 = bf16[4,2,128,768]{3,2,1,0:T(8,128)(2,1)} async-done(((bf16[4,2,128,768]{3,2,1,0:T(8,128)(2,1)}), bf16[4,2,128,768]{3,2,1,0:T(8,128)(2,1)}, u32[]{:S(2)}, u32[]{:S(2)}) %all-to-all-start.2) | async-done | bytes 1572896 | tf_op jit(solution)/shard_map/all_to_all | solution.py:232
  376.3 11.7 %gather_fusion.4 = bf16[2048,768]{1,0:T(8,128)(2,1)} fusion(bf16[1024,768]{1,0:T(8,128)(2,1)} %bitcast.81, s32[2048]{0:T(1024)S(1)} %broadcast_clamp_fusion), kind=kCustom, calls=%fused_computation.4 | custom fusion | bytes 6299648 | tf_op jit(solution)/shard_map/gather | solution.py:240
  395.8 11.2 %multiply_reduce_fusion.3 = f32[1024,768]{1,0:T(8,128)} fusion(f32[1024,2,768]{2,1,0:T(2,128)} %reshape.554, f32[1024,2]{1,0:T(8,128)} %copy.195), kind=kLoop, calls=%fused_computation.74 | loop fusion | flops 2359296 | bytes 9445376 | tf_op jit(solution)/shard_map/reduce_sum | solution.py:239
  418.3 17.3 %multiply_reduce_fusion.2 = (f32[1024,2]{1,0:T(8,128)}, f32[1024,768]{1,0:T(8,128)}) fusion(f32[1024,2,768]{2,1,0:T(2,128)} %reshape.553, f32[1024,768]{1,0:T(8,128)} %copy.199, f32[1024,2]{1,0:T(8,128)} %copy.186), kind=kLoop, calls=%fused_computation.73 | loop fusion | flops 5502976 | bytes 12599296 | tf_op jit(solution)/shard_map/reduce_sum | solution.py:197
  463.6 18.8 %multiply_reduce_fusion.1 = (f32[12,512]{1,0:T(8,128)}, f32[12,512,1024]{2,1,0:T(8,128)}) fusion(f32[12,512]{1,0:T(8,128)} %log_add_fusion.1, f32[12,512,1024]{2,1,0:T(8,128)} %get-tuple-element.117, pred[512,1024]{1,0:T(8,128)(4,1)} %get-tuple-element.112, bf16[512,12,64]{0,2,1:T(8,128)(2,1)} %bitcast.435, bf16[1024,12,64]{0,2,1:T(8,128)(2,1)} %bitcast.425), kind=kOutput, calls=%fused_computation.13 | convolution fusion | flops 836757504 | bytes 53264384 | tf_op jit(solution)/shard_map/qhd,khd->hqk/dot_general | solution.py:262
  482.5 22.7 %multiply_convert_fusion.1 = bf16[12,512,1024]{2,1,0:T(8,128)(2,1)} fusion(f32[12,512,1024]{2,1,0:T(8,128)} %get-tuple-element.122, f32[12,512]{1,0:T(8,128)} %get-tuple-element.121, f32[12,512]{1,0:T(8,128)} %log_add_fusion.1, f32[12,512,1024]{2,1,0:T(8,128)} %get-tuple-element.117, pred[512,1024]{1,0:T(8,128)(4,1)} %get-tuple-element.112), kind=kLoop, calls=%fused_computation.12 | loop fusion | flops 37748736 | bytes 63488000 | tf_op jit(solution)/shard_map/convert_element_type | solution.py:265
  505.2 9.5 fusion.123
  514.7 8.6 fusion.198
  523.3 13.1 %fusion.4 = f32[12,64,1024]{2,1,0:T(8,128)} fusion(bf16[512,12,64]{0,2,1:T(8,128)(2,1)S(1)} %bitcast.438, f32[12,512]{1,0:T(8,128)S(1)} %copy-done.37, f32[12,512,1024]{2,1,0:T(8,128)} %get-tuple-element.115, pred[512,1024]{1,0:T(8,128)(4,1)S(1)} %copy-done.18), kind=kOutput, calls=%fused_computation.25 | convolution fusion | flops 830472192 | bytes 29646848 | tf_op jit(solution)/shard_map/hqk,qhd->khd/dot_general | solution.py:277
  536.4 18.8 %multiply_reduce_fusion = (f32[12,512]{1,0:T(8,128)}, f32[12,512,1024]{2,1,0:T(8,128)}) fusion(f32[12,512]{1,0:T(8,128)} %log_add_fusion, f32[12,512,1024]{2,1,0:T(8,128)} %get-tuple-element.115, pred[512,1024]{1,0:T(8,128)(4,1)} %copy-done.17, bf16[512,12,64]{0,2,1:T(8,128)(2,1)} %bitcast.437, bf16[1024,12,64]{0,2,1:T(8,128)(2,1)} %bitcast.426), kind=kOutput, calls=%fused_computation.10 | convolution fusion | flops 836757504 | bytes 53264384 | tf_op jit(solution)/shard_map/qhd,khd->hqk/dot_general | solution.py:262
  555.2 13.2 %add_convert_fusion = bf16[12,64,1024]{2,1,0:T(8,128)(2,1)S(1)} fusion(f32[12,64,1024]{2,1,0:T(8,128)} %fusion.4, bf16[512,12,64]{0,2,1:T(8,128)(2,1)} %bitcast.436, f32[12,512]{1,0:T(8,128)} %log_add_fusion.1, f32[12,512,1024]{2,1,0:T(8,128)} %get-tuple-element.117, pred[512,1024]{1,0:T(8,128)(4,1)} %get-tuple-element.112), kind=kOutput, calls=%fused_computation.123 | convolution fusion | flops 832045056 | bytes 31219712 | tf_op jit(solution)/shard_map/hqk,qhd->khd/dot_general | solution.py:277
  568.5 21.8 %multiply_convert_fusion = bf16[12,512,1024]{2,1,0:T(8,128)(2,1)} fusion(f32[12,512,1024]{2,1,0:T(8,128)} %get-tuple-element.124, f32[12,512]{1,0:T(8,128)S(1)} %copy-done.43, f32[12,512]{1,0:T(8,128)S(1)} %copy-done.38, f32[12,512,1024]{2,1,0:T(8,128)} %get-tuple-element.115, pred[512,1024]{1,0:T(8,128)(4,1)S(1)} %copy-done.19), kind=kLoop, calls=%fused_computation.9 | loop fusion | flops 37748736 | bytes 63488000 | tf_op jit(solution)/shard_map/convert_element_type | solution.py:265
  590.4 8.7 fusion.124
  615.7 9.9 %convolution_bitcast_fusion = f32[1,3072,768]{2,1,0:T(8,128)} fusion(f32[4,128,3072]{2,1,0:T(8,128)} %fusion.44, bf16[4,2,128,768]{3,2,1,0:T(8,128)(2,1)} %all-to-all-done.1), kind=kOutput, calls=%fused_computation.79 | convolution fusion | flops 2430074880 | bytes 16515072 | tf_op jit(solution)/shard_map/slcf,slcd->lfd/dot_general | solution.py:223
  638.0 8.7 fusion.196
  665.5 40.6 %all-reduce = (f32[768]{0:T(1024)}, f32[768]{0:T(1024)}, f32[768]{0:T(1024)}, f32[768]{0:T(1024)}, f32[768,8]{0,1:T(8,128)}) all-reduce(f32[768]{0:T(1024)} %get-tuple-element.81, f32[768]{0:T(1024)} %get-tuple-element.125, f32[768]{0:T(1024)} %get-tuple-element.77, ...), channel_id=1, replica_groups=mesh['expert'=4,'batch'=8] {'expert','batch'}, use_global_device_ids=true, to_apply=%region_28.29 | all-reduce | flops 9216 | bytes 73728 | tf_op jit(solution)/shard_map/psum | solution.py:296
  706.1 100.4 %all-reduce.4.cloned.1.call-done = (f32[768,2304]{1,0:T(8,128)}, f32[768,768]{1,0:T(8,128)}) async-done(((f32[768,2304]{1,0:T(8,128)}, f32[768,768]{1,0:T(8,128)}), (f32[768,2304]{1,0:T(8,128)}, f32[768,768]{1,0:T(8,128)})) %all-reduce.4.cloned.1.call-update) | async-done | bytes 9437200 | tf_op jit(solution)/shard_map/psum | solution.py:296
  806.5 80.8 %reduce-scatter.5.cloned.1.call-done = f32[1,384,768]{2,1,0:T(8,128)} async-done(((f32[1,3072,768]{2,1,0:T(8,128)}), f32[1,384,768]{2,1,0:T(8,128)}) %reduce-scatter.5.cloned.1.call-update) | async-done | bytes 1179664 | tf_op jit(solution)/shard_map/reduce_scatter | solution.py:237
  887.3 80.9 %reduce-scatter.3.cloned.1.call-done = f32[1,96,3072]{2,1,0:T(8,128)} async-done(((f32[1,768,3072]{2,1,0:T(8,128)}), f32[1,96,3072]{2,1,0:T(8,128)}) %reduce-scatter.3.cloned.1.call-update) | async-done | bytes 1179664 | tf_op jit(solution)/shard_map/reduce_scatter | solution.py:236
  (305 shorter events, 311.0 us)
Async XLA Ops:
  7.2 253.4 %all-gather.9.cloned.1.call-start = ((), (), s32[]{:S(2)}) async-start(), calls=%async_computation.7 | async-start | bytes 5308416 | tf_op jit(solution)/shard_map/all_gather | solution.py:180
  7.9 260.5 %all-gather.5.cloned.1.call-start = ((), (), s32[]{:S(2)}) async-start(), calls=%async_computation.5 | async-start | bytes 5308416 | tf_op jit(solution)/shard_map/all_gather | solution.py:178
  8.7 267.6 %all-gather.11.cloned.1.call-start = ((), (), s32[]{:S(2)}) async-start(), calls=%async_computation.8 | async-start | bytes 5308416 | tf_op jit(solution)/shard_map/all_gather | solution.py:181
  9.4 275.7 %all-gather.7.cloned.1.call-start = ((), (), s32[]{:S(2)}) async-start(), calls=%async_computation.6 | async-start | bytes 5308416 | tf_op jit(solution)/shard_map/all_gather | solution.py:179
  46.1 14.9 %copy-start.17 = (pred[512,1024]{1,0:T(8,128)(4,1)}, pred[512,1024]{1,0:T(8,128)(4,1)S(1)}, u32[]{:S(2)}) copy-start(pred[512,1024]{1,0:T(8,128)(4,1)S(1)} %get-tuple-element.113) | copy-start | bytes 1572868
  61.0 12.5 %copy-start.35 = (f32[12,512]{1,0:T(8,128)}, f32[12,512]{1,0:T(8,128)S(1)}, u32[]{:S(2)}) copy-start(f32[12,512]{1,0:T(8,128)S(1)} %get-tuple-element.114) | copy-start | bytes 73732
  61.0 16.3 %copy-start.1 = (f32[12,512,1024]{2,1,0:T(8,128)S(1)}, f32[12,512,1024]{2,1,0:T(8,128)}, u32[]{:S(2)}) copy-start(f32[12,512,1024]{2,1,0:T(8,128)} %get-tuple-element.115) | copy-start | bytes 75497472
  73.5 13.8 %copy-start.44 = (f32[12,512]{1,0:T(8,128)}, f32[12,512]{1,0:T(8,128)S(1)}, u32[]{:S(2)}) copy-start(f32[12,512]{1,0:T(8,128)S(1)} %fusion.1) | copy-start | bytes 73732
  99.3 14.2 %copy-start.36 = (f32[12,512]{1,0:T(8,128)}, f32[12,512]{1,0:T(8,128)S(1)}, u32[]{:S(2)}) copy-start(f32[12,512]{1,0:T(8,128)S(1)} %get-tuple-element.116) | copy-start | bytes 73732
  99.3 16.5 %copy-start.2 = (f32[12,512,1024]{2,1,0:T(8,128)S(1)}, f32[12,512,1024]{2,1,0:T(8,128)}, u32[]{:S(2)}) copy-start(f32[12,512,1024]{2,1,0:T(8,128)} %get-tuple-element.117) | copy-start | bytes 75497472
  99.3 16.5 %copy-start.20 = (pred[512,1024]{1,0:T(8,128)(4,1)S(1)}, pred[512,1024]{1,0:T(8,128)(4,1)}, u32[]{:S(2)}) copy-start(pred[512,1024]{1,0:T(8,128)(4,1)} %get-tuple-element.112) | copy-start | bytes 1572868
  115.8 13.2 %copy-start.67 = (s32[1,8,2,128]{3,1,2,0:T(8,128)S(1)}, s32[1,8,2,128]{3,1,2,0:T(8,128)}, u32[]{:S(2)}) copy-start(s32[1,8,2,128]{3,1,2,0:T(8,128)} %copy.226) | copy-start | bytes 24580
  146.6 30.1 %copy-start.68 = (pred[4,2,128]{2,1,0:T(4,128)(4,1)}, pred[4,2,128]{2,1,0:T(4,128)(4,1)S(1)}, u32[]{:S(2)}) copy-start(pred[4,2,128]{2,1,0:T(4,128)(4,1)S(1)} %broadcast_in_dim.157) | copy-start | bytes 3076
  179.6 75.1 %collective-permute-start.2 = (bf16[1,2,128,768]{3,2,1,0:T(8,128)(2,1)}, bf16[1,2,128,768]{3,2,1,0:T(8,128)(2,1)}, u32[]{:S(2)}, u32[]{:S(2)}) collective-permute-start(bf16[1,2,128,768]{3,2,1,0:T(8,128)(2,1)} %get-tuple-element.109), channel_id=1, source_target_pairs={{0,24},{8,16},{16,8},{24,0},{1,25},{9,17},{17,9},{25,1},{2,26},{10... | collective-permute-start | bytes 1179656 | tf_op jit(solution)/shard_map/ppermute | solution.py:174
  184.2 70.4 %collective-permute-start.1 = (bf16[1,2,128,768]{3,2,1,0:T(8,128)(2,1)}, bf16[1,2,128,768]{3,2,1,0:T(8,128)(2,1)}, u32[]{:S(2)}, u32[]{:S(2)}) collective-permute-start(bf16[1,2,128,768]{3,2,1,0:T(8,128)(2,1)} %get-tuple-element.110), channel_id=1, source_target_pairs={{0,16},{8,24},{16,0},{24,8},{1,17},{9,25},{17,1},{25,9},{2,18},{10... | collective-permute-start | bytes 1179656 | tf_op jit(solution)/shard_map/ppermute | solution.py:174
  184.2 70.4 %collective-permute-start = (bf16[1,2,128,768]{3,2,1,0:T(8,128)(2,1)}, bf16[1,2,128,768]{3,2,1,0:T(8,128)(2,1)}, u32[]{:S(2)}, u32[]{:S(2)}) collective-permute-start(bf16[1,2,128,768]{3,2,1,0:T(8,128)(2,1)} %get-tuple-element.111), channel_id=1, source_target_pairs={{0,8},{8,0},{16,24},{24,16},{1,9},{9,1},{17,25},{25,17},{2,10},{10... | collective-permute-start | bytes 1179656 | tf_op jit(solution)/shard_map/ppermute | solution.py:174
  249.3 45.1 %all-to-all-start.1 = ((bf16[4,2,128,768]{3,2,1,0:T(8,128)(2,1)}), bf16[4,2,128,768]{3,2,1,0:T(8,128)(2,1)}, u32[]{:S(2)}, u32[]{:S(2)}) async-start(bf16[4,2,128,768]{3,2,1,0:T(8,128)(2,1)} %fusion.85), calls=%async_computation.1 | async-start | bytes 3145728 | tf_op jit(solution)/shard_map/all_to_all | solution.py:210
  294.5 40.9 %all-to-all-start = ((bf16[4,2,128,768]{3,2,1,0:T(8,128)(2,1)}), bf16[4,2,128,768]{3,2,1,0:T(8,128)(2,1)}, u32[]{:S(2)}, u32[]{:S(2)}) async-start(bf16[4,2,128,768]{3,2,1,0:T(8,128)(2,1)} %copy.191), calls=%async_computation | async-start | bytes 3145728 | tf_op jit(solution)/shard_map/all_to_all | solution.py:190
  332.3 12.8 %copy-start.42 = (pred[2,1024]{1,0:T(4,128)(4,1)S(1)}, pred[2,1024]{1,0:T(4,128)(4,1)}, u32[]{:S(2)}) copy-start(pred[2,1024]{1,0:T(4,128)(4,1)} %copy-done.41) | copy-start | bytes 6148
  332.3 12.8 %copy-start.53 = (f32[1024]{0:T(1024)S(1)}, f32[1024]{0:T(1024)}, u32[]{:S(2)}) copy-start(f32[1024]{0:T(1024)} %copy-done.52) | copy-start | bytes 12292
  335.3 41.0 %all-to-all-start.2 = ((bf16[4,2,128,768]{3,2,1,0:T(8,128)(2,1)}), bf16[4,2,128,768]{3,2,1,0:T(8,128)(2,1)}, u32[]{:S(2)}, u32[]{:S(2)}) async-start(bf16[4,2,128,768]{3,2,1,0:T(8,128)(2,1)} %copy.202), calls=%async_computation.2 | async-start | bytes 3145728 | tf_op jit(solution)/shard_map/all_to_all | solution.py:232
  339.7 466.8 %all-reduce.4.cloned.1.call-start = ((), (), s32[]{:S(2)}) async-start(), calls=%async_computation.11 | async-start | bytes 18874368 | tf_op jit(solution)/shard_map/psum | solution.py:296
  418.3 20.6 %copy-start.34 = (s32[1,1024,2]{1,2,0:T(2,128)S(1)}, s32[1,1024,2]{1,2,0:T(2,128)}, u32[]{:S(2)}) copy-start(s32[1,1024,2]{1,2,0:T(2,128)} %param.17) | copy-start | bytes 24580
  418.3 20.6 %copy-start.47 = (f32[1024]{0:T(1024)S(1)}, f32[1024]{0:T(1024)}, u32[]{:S(2)}) copy-start(f32[1024]{0:T(1024)} %copy-done.46) | copy-start | bytes 12292
  482.5 22.7 %copy-start.10 = (bf16[1024,768]{0,1:T(8,128)(2,1)S(1)}, bf16[1024,768]{0,1:T(8,128)(2,1)}, u32[]{:S(2)}) copy-start(bf16[1024,768]{0,1:T(8,128)(2,1)} %copy.182) | copy-start | bytes 4718596
  555.2 13.3 %copy-start.19 = (pred[512,1024]{1,0:T(8,128)(4,1)S(1)}, pred[512,1024]{1,0:T(8,128)(4,1)}, u32[]{:S(2)}) copy-start(pred[512,1024]{1,0:T(8,128)(4,1)} %copy-done.17) | copy-start | bytes 1572868
  555.2 13.3 %copy-start.38 = (f32[12,512]{1,0:T(8,128)S(1)}, f32[12,512]{1,0:T(8,128)}, u32[]{:S(2)}) copy-start(f32[12,512]{1,0:T(8,128)} %log_add_fusion) | copy-start | bytes 73732
  555.2 13.3 %copy-start.43 = (f32[12,512]{1,0:T(8,128)S(1)}, f32[12,512]{1,0:T(8,128)}, u32[]{:S(2)}) copy-start(f32[12,512]{1,0:T(8,128)} %get-tuple-element.123) | copy-start | bytes 73732
  568.5 37.8 %copy-start.76 = (bf16[12,64,1024]{2,1,0:T(8,128)(2,1)}, bf16[12,64,1024]{2,1,0:T(8,128)(2,1)S(1)}, u32[]{:S(2)}) copy-start(bf16[12,64,1024]{2,1,0:T(8,128)(2,1)S(1)} %add_convert_fusion) | copy-start | bytes 4718596
  568.5 21.9 %copy-start.11 = (bf16[1024,768]{0,1:T(8,128)(2,1)S(1)}, bf16[1024,768]{0,1:T(8,128)(2,1)}, u32[]{:S(2)}) copy-start(bf16[1024,768]{0,1:T(8,128)(2,1)} %copy.182) | copy-start | bytes 4718596
  615.7 271.7 %reduce-scatter.5.cloned.1.call-start = ((), (), s32[]{:S(2)}) async-start(), calls=%async_computation.10 | async-start | bytes 10616832 | tf_op jit(solution)/shard_map/reduce_scatter | solution.py:237
  625.6 342.6 %reduce-scatter.3.cloned.1.call-start = ((), (), s32[]{:S(2)}) async-start(), calls=%async_computation.9 | async-start | bytes 10616832 | tf_op jit(solution)/shard_map/reduce_scatter | solution.py:236
  (58 other events, 258.3 us)
Sparse Core Ops, SparseCore 0:
  9.9 41.4 all-gather.8
  53.3 38.7 all-gather.4
  94.0 38.7 all-gather.10
  134.6 38.7 all-gather.6
  615.8 190.6 all-reduce.3
  810.4 76.8 reduce-scatter.4
  891.4 76.8 reduce-scatter.2
